TPU v7x, 32 devices: a whole 2x2x4 slice. The times are simulated.
32 devices in a mesh: dp: 8 (over y, x, core), tensor: 4 (over z).
Axes of the slice: x: 2, y: 2, z: 4, core: 2. Of those that a mesh axis runs over, the one named last changes fastest.
Arguments:
- hidden_in: bfloat16 [32, 512, 768], P('dp'), may hold values from -6 to 6
- out_grad: bfloat16 [32, 512, 768], P('dp'), may hold values from -3 to 3
- segment_ids: int32 [32, 512], P('dp'), may hold values from 0 to 7, never falling along the last dimension, each value on 1 to 256 neighbouring positions
- step_count: int32 [1], replicated, may hold values from 1 to 199999
- qkv_state: float32 [3, 768, 3, 768], P(None, 'dp', None, 'tensor'), as said below
- qv_bias_state: float32 [3, 2, 12, 64], P(None, None, 'tensor', 'dp'), as said below
- out_state: float32 [3, 768, 768], P(None, 'tensor', 'dp'), as said below
- up_state: float32 [3, 768, 3072], P(None, 'dp', 'tensor'), as said below
- up_bias_state: float32 [3, 24, 128], P(None, 'tensor', 'dp'), as said below
- down_state: float32 [3, 3072, 768], P(None, 'tensor', 'dp'), as said below
- vector_state: float32 [3, 6, 768], P(None, None, 'dp'), as said below
Outputs:
- hidden_out: bfloat16 [32, 512, 768], P('dp')
- grad_in: bfloat16 [32, 512, 768], P('dp')
- grad_qkv: float32 [768, 3, 768], P('dp', None, 'tensor')
- grad_qv_bias: float32 [2, 12, 64], P(None, 'tensor', 'dp')
- grad_out: float32 [768, 768], P('tensor', 'dp')
- grad_up: float32 [768, 3072], P('dp', 'tensor')
- grad_up_bias: float32 [24, 128], P('tensor', 'dp')
- grad_down: float32 [3072, 768], P('tensor', 'dp')
- grad_vectors: float32 [6, 768], P(None, 'dp')
- new_qkv_state: float32 [2, 768, 3, 768], P(None, 'dp', None, 'tensor')
- new_qv_bias_state: float32 [2, 2, 12, 64], P(None, None, 'tensor', 'dp')
- new_out_state: float32 [2, 768, 768], P(None, 'tensor', 'dp')
- new_up_state: float32 [2, 768, 3072], P(None, 'dp', 'tensor')
- new_up_bias_state: float32 [2, 24, 128], P(None, 'tensor', 'dp')
- new_down_state: float32 [2, 3072, 768], P(None, 'tensor', 'dp')
- new_vector_state: float32 [2, 6, 768], P(None, None, 'dp')
- plan: float32 [3], replicated
Inputs may be any that keep to these rules, and one draw needn't show every extreme that they name: `segment_ids`: within each packed row the fragment numbers never fall; a token attends exactly to the tokens of its own row with the same number. `qkv_state`: index 2 (second moments) is positive. `qv_bias_state`: index 2 (second moments) is positive. `out_state`: index 2 (second moments) is positive. `up_state`: index 2 (second moments) is positive. `up_bias_state`: index 2 (second moments) is positive. `down_state`: index 2 (second moments) is positive. `vector_state`: index 2 (second moments) is positive.
All inputs are finite; a program needn't handle non-finite values.
Results may differ from a plain program's by a relative error of at most 0.023.
The roundings to bfloat16 on the way count: a program that leaves them out, or rounds other values in their place, can miss the bound.
Values may be sent and summed in bfloat16 or wider, within the bound.
No kernel may reach another device: no remote copies, remote signals or barrier semaphores. Data moves between devices by JAX's collectives and lax.ppermute only.
A program may use at most 192 MiB of HBM per device.

v0:
```python
import math
import jax
import jax.numpy as jnp
from jax import lax
from jax.sharding import PartitionSpec as P

HD = 64
norm_eps = 1e-05
beta_first = 0.9
beta_second = 0.999
warm_steps = 10000.0
total_steps = 200000.0


def layer_norm(value, gain, shift):
    center = value - jnp.mean(value, axis=-1, keepdims=True)
    spread = jnp.mean(center * center, axis=-1, keepdims=True)
    return center * lax.rsqrt(spread + norm_eps) * gain + shift


def gelu_exact(value):
    return 0.5 * value * (1.0 + lax.erf(value * 0.7071067811865476))


def scores_of(query, key_rows, segments):
    raw = jnp.einsum(
        "bqhd,bkhd->bhqk", query, key_rows, preferred_element_type=jnp.float32
    ) * HD ** (-0.5)
    same = segments[:, :, None] == segments[:, None, :]
    return jnp.where(same[:, None], raw, -1e30)


def contract_rows(left, right):
    return lax.dot_general(
        left, right, (((0,), (0,)), ((), ())), preferred_element_type=jnp.float32
    )


def contract_cols(left, right):
    return lax.dot_general(
        left, right, (((1,), (1,)), ((), ())), preferred_element_type=jnp.float32
    )


def moment_update(state, grad):
    moment_one = beta_first * state[1] + (1.0 - beta_first) * grad
    moment_two = beta_second * state[2] + (1.0 - beta_second) * grad * grad
    return jnp.stack([moment_one, moment_two])


def body(
    hidden_in,
    out_grad,
    segment_ids,
    step_count,
    qkv_state,
    qv_bias_state,
    out_state,
    up_state,
    up_bias_state,
    down_state,
    vector_state,
):
    bf = jnp.bfloat16
    fl = jnp.float32
    w_qkv, b_qv, w_out, w_up, b_up, w_down, vectors = (
        lax.all_gather(qkv_state[0].astype(bf), "dp", axis=0, tiled=True),
        lax.all_gather(qv_bias_state[0].astype(bf), "dp", axis=2, tiled=True),
        lax.all_gather(out_state[0].astype(bf), "dp", axis=1, tiled=True),
        lax.all_gather(up_state[0].astype(bf), "dp", axis=0, tiled=True),
        lax.all_gather(up_bias_state[0].astype(bf), "dp", axis=1, tiled=True),
        lax.all_gather(down_state[0].astype(bf), "dp", axis=1, tiled=True),
        lax.all_gather(vector_state[0].astype(bf), "dp", axis=1, tiled=True),
    )
    count, length, width_model = hidden_in.shape
    rows = count * length
    heads_local = b_qv.shape[1]
    head_width = heads_local * HD
    ff_local = w_up.shape[1]
    scale = HD ** (-0.5)
    plain = hidden_in.reshape(rows, width_model)
    cotangent = out_grad.reshape(rows, width_model)
    vec = vectors.astype(fl)
    proj = jnp.einsum("td,dcf->tcf", plain, w_qkv, preferred_element_type=fl)
    bias_f = b_qv.astype(fl).reshape(2, head_width)
    bias = jnp.stack([bias_f[0], jnp.zeros((head_width,), fl), bias_f[1]])
    proj_b = (proj + bias[None]).astype(bf)
    heads = proj_b.reshape(count, length, 3, heads_local, HD)
    query = heads[:, :, 0]
    key_rows = heads[:, :, 1]
    value_rows = heads[:, :, 2]
    scores = scores_of(query, key_rows, segment_ids)
    top = jnp.max(scores, axis=-1, keepdims=True)
    expd = jnp.exp(scores - top)
    denom = jnp.sum(expd, axis=-1, keepdims=True)
    log_total = top + jnp.log(denom)
    probs_b = (expd / denom).astype(bf)
    context = (
        jnp.einsum("bhqk,bkhd->bqhd", probs_b, value_rows, preferred_element_type=fl)
        .astype(bf)
        .reshape(rows, head_width)
    )
    attn_part = jnp.dot(context, w_out, preferred_element_type=fl)
    attn = lax.psum(attn_part.astype(jnp.bfloat16), "tensor").astype(jnp.float32)
    first, first_pull = jax.vjp(layer_norm, plain.astype(fl) + attn + vec[4], vec[0], vec[1])
    first_b = first.astype(bf)
    up = jnp.dot(first_b, w_up, preferred_element_type=fl) + b_up.astype(fl).reshape(ff_local)
    act, gelu_pull = jax.vjp(gelu_exact, up)
    act_b = act.astype(bf)
    ffn_part = jnp.dot(act_b, w_down, preferred_element_type=fl)
    ffn = lax.psum(ffn_part.astype(jnp.bfloat16), "tensor").astype(jnp.float32)
    out, second_pull = jax.vjp(layer_norm, first + ffn + vec[5], vec[2], vec[3])
    grad_r2, grad_g2, grad_b2 = second_pull(cotangent.astype(fl))
    grad_ffn = grad_r2.astype(bf)
    grad_down = contract_rows(act_b, grad_ffn)
    grad_act = contract_cols(grad_ffn, w_down)
    grad_up_b = gelu_pull(grad_act)[0].astype(bf)
    grad_wup = contract_rows(first_b, grad_up_b)
    grad_bup = jnp.sum(grad_up_b, axis=0, dtype=fl).reshape(b_up.shape)
    feed_part = contract_cols(grad_up_b, w_up)
    feed_back = lax.psum(feed_part.astype(jnp.bfloat16), "tensor").astype(jnp.float32)
    grad_first = grad_r2 + feed_back.astype(bf).astype(fl)
    grad_r1, grad_g1, grad_b1 = first_pull(grad_first)
    grad_attn = grad_r1.astype(bf)
    grad_wout = contract_rows(context, grad_attn)
    grad_context = (
        contract_cols(grad_attn, w_out).astype(bf).reshape(count, length, heads_local, HD)
    )
    again = scores_of(query, key_rows, segment_ids)
    probs = jnp.exp(again - log_total)
    probs_again = probs.astype(bf)
    grad_probs = jnp.einsum("bqhd,bkhd->bhqk", grad_context, value_rows, preferred_element_type=fl)
    grad_value = jnp.einsum("bhqk,bqhd->bkhd", probs_again, grad_context, preferred_element_type=fl)
    row_dot = jnp.sum(probs * grad_probs, axis=-1, keepdims=True)
    grad_scores = (probs * (grad_probs - row_dot)).astype(bf)
    grad_query = (
        jnp.einsum("bhqk,bkhd->bqhd", grad_scores, key_rows, preferred_element_type=fl) * scale
    )
    grad_key = jnp.einsum("bhqk,bqhd->bkhd", grad_scores, query, preferred_element_type=fl) * scale
    grad_proj = (
        jnp.stack([grad_query, grad_key, grad_value], axis=2)
        .astype(bf)
        .reshape(rows, 3, head_width)
    )
    proj_sums = jnp.sum(grad_proj, axis=0, dtype=fl)
    grad_bqv = jnp.stack([proj_sums[0], proj_sums[2]]).reshape(2, heads_local, HD)
    grad_wqkv = jnp.einsum("td,tcf->dcf", plain, grad_proj, preferred_element_type=fl)
    input_part = jnp.einsum("tcf,dcf->td", grad_proj, w_qkv, preferred_element_type=fl)
    vec_part = jnp.stack(
        [grad_g1, grad_b1, grad_g2, grad_b2, jnp.sum(grad_r1, axis=0), jnp.sum(grad_r2, axis=0)]
    )
    input_back = lax.psum(input_part.astype(jnp.bfloat16), "tensor").astype(jnp.float32)
    grad_in = (grad_r1 + input_back.astype(bf).astype(fl)).astype(bf).reshape(hidden_in.shape)
    hidden_out = out.astype(bf).reshape(hidden_in.shape)
    summed = (
        lax.psum_scatter(grad_wqkv, "dp", scatter_dimension=0, tiled=True),
        lax.psum_scatter(grad_bqv, "dp", scatter_dimension=2, tiled=True),
        lax.psum_scatter(grad_wout, "dp", scatter_dimension=1, tiled=True),
        lax.psum_scatter(grad_wup, "dp", scatter_dimension=0, tiled=True),
        lax.psum_scatter(grad_bup, "dp", scatter_dimension=1, tiled=True),
        lax.psum_scatter(grad_down, "dp", scatter_dimension=1, tiled=True),
        lax.psum_scatter(vec_part, "dp", scatter_dimension=1, tiled=True),
    )
    steps_f = step_count[0].astype(fl)
    factor = jnp.minimum(steps_f / warm_steps, (total_steps - steps_f) / (total_steps - warm_steps))
    fix_first = 1.0 - jnp.exp(steps_f * math.log(beta_first))
    fix_second = 1.0 - jnp.exp(steps_f * math.log(beta_second))
    states = (
        qkv_state,
        qv_bias_state,
        out_state,
        up_state,
        up_bias_state,
        down_state,
        vector_state,
    )
    news = tuple((moment_update(s, g) for s, g in zip(states, summed)))
    plan = jnp.stack([factor, fix_first, fix_second])
    return (
        hidden_out,
        grad_in,
        summed[0],
        summed[1],
        summed[2],
        summed[3],
        summed[4],
        summed[5],
        summed[6],
        news[0],
        news[1],
        news[2],
        news[3],
        news[4],
        news[5],
        news[6],
        plan,
    )


def solution(mesh):
    return jax.shard_map(
        body,
        mesh=mesh,
        in_specs=(
            P("dp", None, None),
            P("dp", None, None),
            P("dp", None),
            P(),
            P(None, "dp", None, "tensor"),
            P(None, None, "tensor", "dp"),
            P(None, "tensor", "dp"),
            P(None, "dp", "tensor"),
            P(None, "tensor", "dp"),
            P(None, "tensor", "dp"),
            P(None, None, "dp"),
        ),
        out_specs=(
            P("dp", None, None),
            P("dp", None, None),
            P("dp", None, "tensor"),
            P(None, "tensor", "dp"),
            P("tensor", "dp"),
            P("dp", "tensor"),
            P("tensor", "dp"),
            P("tensor", "dp"),
            P(None, "dp"),
            P(None, "dp", None, "tensor"),
            P(None, None, "tensor", "dp"),
            P(None, "tensor", "dp"),
            P(None, "dp", "tensor"),
            P(None, "tensor", "dp"),
            P(None, "tensor", "dp"),
            P(None, None, "dp"),
            P(),
        ),
        check_vma=False,
    )
```

profile of v0, /device:TPU:0, one launch (start us, length us, event | category | flops | bytes accessed | tf_op | source)
XLA Modules:
  0.0 760.8 jit_solution(6386560561636301362)
XLA Ops:
  9.0 10.6 %all-gather.1 = bf16[1,2,3,64]{2,1,0,3:T(2,128)(2,1)S(1)} all-gather(bf16[1,2,3,8]{2,1,0,3:T(2,128)(2,1)S(1)} %copy.181), channel_id=3, replica_groups=mesh['dp'=8,'tensor'=4] {'dp'}, dimensions={3}, use_global_device_ids=true | all-gather | bytes 864 | tf_op jit(solution)/shard_map/all_gather | solution.py:68
  22.8 11.3 %all-gather.2 = bf16[1,192,768]{1,0,2:T(2,128)(2,1)} all-gather(bf16[1,192,96]{1,0,2:T(2,128)(2,1)S(1)} %copy.142), channel_id=4, replica_groups=mesh['dp'=8,'tensor'=4] {'dp'}, dimensions={2}, use_global_device_ids=true | all-gather | bytes 331776 | tf_op jit(solution)/shard_map/all_gather | solution.py:69
  34.1 2.2 copy.143
  36.3 2.3 broadcast_compare_fusion
  38.6 15.8 %all-gather = bf16[1,768,3,192]{3,2,0,1:T(4,128)(2,1)} all-gather(bf16[1,96,3,192]{3,2,0,1:T(4,128)(2,1)} %copy.132), channel_id=2, replica_groups=mesh['dp'=8,'tensor'=4] {'dp'}, dimensions={1}, use_global_device_ids=true | all-gather | bytes 995328 | tf_op jit(solution)/shard_map/all_gather | solution.py:67
  54.4 3.4 copy.133
  57.9 3.2 fusion.74
  61.2 1.7 add_convert_fusion.5
  62.9 6.2 reshape.215
  69.1 2.4 fusion.69
  71.5 4.4 fusion.73
  76.0 1.8 fusion
  77.8 2.8 copy-done
  80.7 2.3 fusion.22
  84.7 2.7 convolution_convert_fusion.2
  87.5 1.6 slice.205
  89.3 1.6 slice.204
  93.2 8.7 %all-gather.5 = bf16[1,6,128]{1,0,2:T(2,128)(2,1)S(1)} all-gather(bf16[1,6,16]{1,0,2:T(2,128)(2,1)} %copy.145), channel_id=7, replica_groups=mesh['dp'=8,'tensor'=4] {'dp'}, dimensions={2}, use_global_device_ids=true | all-gather | bytes 1728 | tf_op jit(solution)/shard_map/all_gather | solution.py:71
  103.2 10.8 %all-gather.3 = bf16[1,6,768]{1,0,2:T(2,128)(2,1)S(1)} all-gather(bf16[1,6,96]{1,0,2:T(2,128)(2,1)S(1)} %copy.185), channel_id=5, replica_groups=mesh['dp'=8,'tensor'=4] {'dp'}, dimensions={2}, use_global_device_ids=true | all-gather | bytes 10368 | tf_op jit(solution)/shard_map/all_gather | solution.py:73
  114.4 13.0 %slice_reduce_fusion.1 = (f32[768]{0:T(1024)S(1)}, f32[768]{0:T(1024)S(1)}, f32[768]{0:T(1024)S(1)}, f32[768]{0:T(1024)S(1)}, f32[768]{0:T(1024)S(1)}, /*index=5*/f32[768]{0:T(1024)S(1)}) fusion(f32[1,6,768]{1,0,2:T(1,128)S(1)} %convert_element_type.169), kind=kLoop, calls=%fused_computation.78 | loop fusion | bytes 36864 | tf_op jit(solution)/shard_map/slice | solution.py:112
  127.4 81.6 %all-reduce.6.cloned.1.call-done = bf16[2048,768]{1,0:T(8,128)(2,1)} async-done(((bf16[2048,768]{1,0:T(8,128)(2,1)}), bf16[2048,768]{1,0:T(8,128)(2,1)}) %all-reduce.6.cloned.1.call-update) | async-done | bytes 3145744 | tf_op jit(solution)/shard_map/psum | solution.py:104
  209.0 3.1 fusion.11
  212.1 3.7 multiply_reduce_fusion.4
  215.8 7.4 multiply_convert_fusion.1
  223.3 6.2 convolution_convert_fusion.1
  229.7 120.0 %all-reduce.8.cloned.1.call-done = bf16[2048,768]{1,0:T(8,128)(2,1)} async-done(((bf16[2048,768]{1,0:T(8,128)(2,1)}), bf16[2048,768]{1,0:T(8,128)(2,1)}) %all-reduce.8.cloned.1.call-update) | async-done | bytes 3145744 | tf_op jit(solution)/shard_map/psum | solution.py:111
  349.7 4.8 fusion.67
  356.4 3.0 fusion.7
  359.5 4.3 fusion.66
  363.8 5.9 convert_reduce_fusion.1
  369.7 1.7 copy-done.35
  371.5 4.0 convolution_convert_fusion
  376.4 8.0 %fusion.60 = f32[768,768]{0,1:T(8,128)} fusion(bf16[2048,768]{1,0:T(8,128)(2,1)} %copy-done.36, f32[2048,768]{1,0:T(8,128)} %copy-done.2, f32[2048]{0:T(1024)S(1)} %negate_multiply_fusion.1), kind=kOutput, calls=%fused_computation.147 | convolution fusion | flops 2419064832 | bytes 11804672 | tf_op jit(solution)/shard_map/dot_general | solution.py:34
  384.5 8.0 %fusion.61 = f32[768,768]{1,0:T(8,128)} fusion(bf16[2048,768]{1,0:T(8,128)(2,1)} %copy-done.35, f32[2048,768]{1,0:T(8,128)} %get-tuple-element.123, f32[768]{0:T(1024)} %copy-done.24, f32[768]{0:T(1024)} %copy-done.22, f32[2048]{0:T(1024)S(1)} %fusion.49), kind=kOutput, calls=%fused_computation.148 | convolution fusion | flops 2422210560 | bytes 11810816 | tf_op jit(solution)/shard_map/dot_general | solution.py:34
  392.8 102.9 %all-reduce.10.cloned.1.call-done = bf16[2048,768]{1,0:T(8,128)(2,1)} async-done(((bf16[2048,768]{1,0:T(8,128)(2,1)}), bf16[2048,768]{1,0:T(8,128)(2,1)}) %all-reduce.10.cloned.1.call-update) | async-done | bytes 3145744 | tf_op jit(solution)/shard_map/psum | solution.py:121
  495.7 8.0 %multiply_reduce_fusion.1 = (f32[768]{0:T(1024)}, f32[2048]{0:T(1024)S(1)}, f32[768]{0:T(1024)}, f32[768]{0:T(1024)}) fusion(f32[2048,768]{1,0:T(8,128)} %get-tuple-element.123, f32[2048]{0:T(1024)S(1)} %fusion.49, bf16[2048,768]{1,0:T(8,128)(2,1)} %all-reduce.10.cloned.1.call-done, f32[2048,768]{1,0:T(8,128)} %copy-done.2, ...), kind=kLoop, calls=%fused_computation.19 | loop fusion | flops 17297152 | bytes 15765504 | tf_op jit(solution)/shard_map/transpose(jvp())/reduce_sum | solution.py:18
  503.7 6.1 fusion.65
  509.8 2.6 copy-done.3
  512.4 2.2 convolution_convert_fusion.3
  514.7 3.0 reshape.218
  517.6 8.3 %multiply_reduce_fusion = (f32[4,3,512]{2,1,0:T(4,128)S(1)}, f32[4,3,512,512]{2,3,1,0:T(8,128)S(1)}) fusion(f32[4,3,512,512]{2,3,1,0:T(8,128)} %copy-done, f32[4,3,512]{2,1,0:T(4,128)S(1)} %log_add_fusion, bf16[4,512,1,3,64]{1,0,4,3,2:T(4,128)(2,1)} %copy-done.11, bf16[4,512,3,64]{1,0,3,2:T(4,128)(2,1)} %reshape.218), kind=kOutput, calls=%fused_computation.1 | convolution fusion | flops 412084224 | bytes 26787840 | tf_op jit(solution)/shard_map/bqhd,bkhd->bhqk/dot_general | solution.py:132
  526.0 6.9 multiply_convert_fusion
  532.9 2.6 copy-done.1
  536.6 1.5 copy.149
  538.1 3.2 stack.101
  541.3 5.1 fusion.21
  546.3 1.5 copy.151
  547.8 2.8 stack.102
  550.6 2.1 constant_dynamic-update-slice_fusion.2
  552.8 5.6 convolution_bitcast_fusion
  558.4 7.7 %fusion.17 = bf16[4,512,3,64]{1,3,2,0:T(8,128)(2,1)} fusion(f32[4,3,512,512]{2,3,1,0:T(8,128)} %copy-done, f32[4,3,512]{2,1,0:T(4,128)S(1)} %log_add_fusion, bf16[4,512,3,64]{1,0,3,2:T(4,128)(2,1)} %reshape.218), kind=kOutput, calls=%fused_computation.53 | convolution fusion | flops 409337856 | bytes 14180352 | tf_op jit(solution)/shard_map/bhqk,bqhd->bkhd/dot_general | solution.py:133
  566.2 2.1 constant_dynamic-update-slice_fusion.1
  568.3 2.6 copy.154
  570.9 2.8 stack.103
  573.7 2.1 constant_dynamic-update-slice_fusion
  575.8 5.8 fusion.75
  581.7 2.8 copy.179
  585.8 6.2 bitcast_convert_fusion
  595.1 1.2 dynamic-slice
  601.6 14.3 %all-reduce = f32[2,3,64]{2,1,0:T(4,128)S(1)} all-reduce(f32[2,3,64]{2,1,0:T(4,128)S(1)} %reshape.220), channel_id=10, replica_groups=mesh['dp'=8,'tensor'=4] {'dp'}, use_global_device_ids=true, to_apply=%region_17.18.clone | all-reduce | flops 384 | bytes 3072
  623.8 19.7 %reduce-scatter.20.cloned.1.call-done = f32[96,576]{1,0:T(8,128)} async-done(((f32[768,576]{1,0:T(8,128)}), f32[96,576]{1,0:T(8,128)}) %reduce-scatter.20.cloned.1.call-update) | async-done | bytes 221200
  644.8 67.8 %all-reduce.12.cloned.1.call-done = bf16[2048,768]{1,0:T(8,128)(2,1)} async-done(((bf16[2048,768]{1,0:T(8,128)(2,1)}), bf16[2048,768]{1,0:T(8,128)(2,1)}) %all-reduce.12.cloned.1.call-update) | async-done | bytes 3145744 | tf_op jit(solution)/shard_map/psum | solution.py:152
  712.5 5.4 add_reduce_fusion
  721.0 31.0 %reduce-scatter.26.cloned.1.call-done = f32[96,6]{1,0:T(8,128)} async-done(((f32[768,6]{1,0:T(8,128)}), f32[96,6]{1,0:T(8,128)}) %reduce-scatter.26.cloned.1.call-update) | async-done | bytes 2320
  (180 shorter events, 36.6 us)
Async XLA Ops:
  8.0 49.9 %copy-start.6 = (bf16[4,512,768]{2,1,0:T(8,128)(2,1)S(1)}, bf16[4,512,768]{2,1,0:T(8,128)(2,1)}, u32[]{:S(2)}) copy-start(bf16[4,512,768]{2,1,0:T(8,128)(2,1)} %param.11) | copy-start | bytes 9437188
  8.0 200.9 %all-reduce.6.cloned.1.call-start = ((), (), s32[]{:S(2)}) async-start(), calls=%async_computation.6 | async-start | bytes 6291456 | tf_op jit(solution)/shard_map/psum | solution.py:104
  71.5 4.4 copy-start.9
  71.5 4.4 copy-start.12
  71.5 6.3 copy-start.11
  76.0 4.7 copy-start
  76.0 4.7 copy-start.16
  77.8 5.3 copy-start.18
  83.9 0.9 copy-start.8
  87.5 128.3 %all-gather.10.cloned.1.call-start = ((), (), s32[]{:S(2)}) async-start(), calls=%async_computation.12 | async-start | bytes 1327104 | tf_op jit(solution)/shard_map/all_gather | solution.py:70
  89.2 134.1 %all-gather.12.cloned.1.call-start = ((), (), s32[]{:S(2)}) async-start(), calls=%async_computation.13 | async-start | bytes 1327104 | tf_op jit(solution)/shard_map/all_gather | solution.py:72
  90.9 258.8 %all-reduce.8.cloned.1.call-start = ((), (), s32[]{:S(2)}) async-start(), calls=%async_computation.7 | async-start | bytes 6291456 | tf_op jit(solution)/shard_map/psum | solution.py:111
  127.3 222.4 %copy-start.22 = (f32[768]{0:T(1024)}, f32[768]{0:T(1024)S(1)}, u32[]{:S(2)}) copy-start(f32[768]{0:T(1024)S(1)} %get-tuple-element.111) | copy-start | bytes 9220
  127.3 222.4 %copy-start.24 = (f32[768]{0:T(1024)}, f32[768]{0:T(1024)S(1)}, u32[]{:S(2)}) copy-start(f32[768]{0:T(1024)S(1)} %get-tuple-element.110) | copy-start | bytes 9220
  208.9 3.2 copy-start.7
  215.8 7.5 copy-start.20
  223.3 6.2 copy-start.36
  229.5 266.2 %all-reduce.10.cloned.1.call-start = ((), (), s32[]{:S(2)}) async-start(), calls=%async_computation.8 | async-start | bytes 6291456 | tf_op jit(solution)/shard_map/psum | solution.py:121
  354.5 1.9 copy-start.4
  356.4 7.4 slice-start
  359.4 4.3 copy-start.34
  359.4 4.3 slice-start.1
  363.8 6.0 copy-start.2
  363.8 7.7 %copy-start.33 = (bf16[1,768,768]{2,1,0:T(8,128)(2,1)S(1)}, bf16[1,768,768]{2,1,0:T(8,128)(2,1)}, u32[]{:S(2)}) copy-start(bf16[1,768,768]{2,1,0:T(8,128)(2,1)} %all-gather.10.cloned.1.call-done) | copy-start | bytes 3538948
  369.7 1.8 copy-start.35
  375.5 222.1 %reduce-scatter.24.cloned.1.call-start = ((), (), s32[]{:S(2)}) async-start(), calls=%async_computation.16 | async-start | bytes 73728
  376.3 8.1 %copy-start.17 = (f32[4,3,512]{2,1,0:T(4,128)S(1)}, f32[4,3,512]{2,1,0:T(4,128)}, u32[]{:S(2)}) copy-start(f32[4,3,512]{2,1,0:T(4,128)} %copy-done.16) | copy-start | bytes 73732
  376.4 8.1 %copy-start.19 = (f32[4,3,512]{2,1,0:T(4,128)S(1)}, f32[4,3,512]{2,1,0:T(4,128)}, u32[]{:S(2)}) copy-start(f32[4,3,512]{2,1,0:T(4,128)} %copy-done.18) | copy-start | bytes 73732
  376.4 241.5 %reduce-scatter.18.cloned.1.call-start = ((), (), s32[]{:S(2)}) async-start(), calls=%async_computation.11 | async-start | bytes 2654208 | tf_op jit(solution)/shard_map/reduce_scatter | solution.py:161
  384.4 235.6 %reduce-scatter.16.cloned.1.call-start = ((), (), s32[]{:S(2)}) async-start(), calls=%async_computation.10 | async-start | bytes 2654208 | tf_op jit(solution)/shard_map/reduce_scatter | solution.py:159
  384.5 111.2 %copy-start.23 = (f32[768]{0:T(1024)S(1)}, f32[768]{0:T(1024)}, u32[]{:S(2)}) copy-start(f32[768]{0:T(1024)} %copy-done.22) | copy-start | bytes 9220
  392.5 111.2 %copy-start.21 = (f32[2048]{0:T(1024)S(1)}, f32[2048]{0:T(1024)}, u32[]{:S(2)}) copy-start(f32[2048]{0:T(1024)} %copy-done.20) | copy-start | bytes 24580
  392.6 229.5 %reduce-scatter.22.cloned.1.call-start = ((), (), s32[]{:S(2)}) async-start(), calls=%async_computation.15 | async-start | bytes 884736
  495.7 8.0 %copy-start.5 = (bf16[2048,768]{1,0:T(8,128)(2,1)S(1)}, bf16[2048,768]{1,0:T(8,128)(2,1)}, u32[]{:S(2)}) copy-start(bf16[2048,768]{1,0:T(8,128)(2,1)} %all-reduce.10.cloned.1.call-done) | copy-start | bytes 9437188
  509.8 2.6 copy-start.3
  526.0 9.5 %copy-start.13 = (bf16[4,512,1,3,64]{1,0,4,3,2:T(4,128)(2,1)S(1)}, bf16[4,512,1,3,64]{1,0,4,3,2:T(4,128)(2,1)}, u32[]{:S(2)}) copy-start(bf16[4,512,1,3,64]{1,0,4,3,2:T(4,128)(2,1)} %copy-done.12) | copy-start | bytes 2359300
  532.9 2.6 copy-start.1
  566.2 77.4 %reduce-scatter.20.cloned.1.call-start = ((), (), s32[]{:S(2)}) async-start(), calls=%async_computation.14 | async-start | bytes 2211840
  584.5 128.0 %all-reduce.12.cloned.1.call-start = ((), (), s32[]{:S(2)}) async-start(), calls=%async_computation.9 | async-start | bytes 6291456 | tf_op jit(solution)/shard_map/psum | solution.py:152
  585.8 8.3 %copy-start.27 = (f32[768]{0:T(1024)S(1)}, f32[768]{0:T(1024)}, u32[]{:S(2)}) copy-start(f32[768]{0:T(1024)} %convert_reduce_fusion) | copy-start | bytes 9220
  585.8 11.7 %copy-start.25 = (f32[768]{0:T(1024)S(1)}, f32[768]{0:T(1024)}, u32[]{:S(2)}) copy-start(f32[768]{0:T(1024)} %get-tuple-element.104) | copy-start | bytes 9220
  585.8 15.2 %copy-start.26 = (f32[768]{0:T(1024)S(1)}, f32[768]{0:T(1024)}, u32[]{:S(2)}) copy-start(f32[768]{0:T(1024)} %get-tuple-element.107) | copy-start | bytes 9220
  592.1 9.0 %copy-start.10 = (bf16[2048,3,192]{0,2,1:T(8,128)(2,1)S(1)}, bf16[2048,3,192]{0,2,1:T(8,128)(2,1)}, u32[]{:S(2)}) copy-start(bf16[2048,3,192]{0,2,1:T(8,128)(2,1)} %constant_dynamic-update-slice_fusion) | copy-start | bytes 7077892
  592.1 31.0 %copy-start.15 = (f32[3,192,96]{2,1,0:T(8,128)S(1)}, f32[3,192,96]{2,1,0:T(8,128)}, u32[]{:S(2)}) copy-start(f32[3,192,96]{2,1,0:T(8,128)} %param.17) | copy-start | bytes 663556
  592.1 159.8 %reduce-scatter.26.cloned.1.call-start = ((), (), s32[]{:S(2)}) async-start(), calls=%async_computation.17 | async-start | bytes 442368
  598.4 119.6 %copy-start.28 = (f32[6,16]{1,0:T(8,128)}, f32[6,16]{1,0:T(8,128)S(1)}, u32[]{:S(2)}) copy-start(f32[6,16]{1,0:T(8,128)S(1)} %copy.176) | copy-start | bytes 1156
  616.6 101.3 %copy-start.30 = (f32[2,3,8]{2,0,1:T(2,128)}, f32[2,3,8]{2,0,1:T(2,128)S(1)}, u32[]{:S(2)}) copy-start(f32[2,3,8]{2,0,1:T(2,128)S(1)} %get-tuple-element.115) | copy-start | bytes 580
  623.1 94.8 %copy-start.14 = (f32[192,96]{1,0:T(8,128)}, f32[192,96]{1,0:T(8,128)S(1)}, u32[]{:S(2)}) copy-start(f32[192,96]{1,0:T(8,128)S(1)} %copy.174) | copy-start | bytes 221188
  644.7 73.2 %copy-start.31 = (f32[1,768]{1,0:T(1,128)S(1)}, f32[1,768]{1,0:T(1,128)}, u32[]{:S(2)}) copy-start(f32[1,768]{1,0:T(1,128)} %reshape.225) | copy-start | bytes 9220
  644.7 108.1 %copy-start.32 = (f32[3,6,96]{2,1,0:T(8,128)S(1)}, f32[3,6,96]{2,1,0:T(8,128)}, u32[]{:S(2)}) copy-start(f32[3,6,96]{2,1,0:T(8,128)} %param.21) | copy-start | bytes 20740
  752.8 0.6 copy-start.29
Sparse Core Ops, SparseCore 0:
  87.6 121.2 all-reduce.5
  229.6 120.0 all-reduce.7
  375.6 120.0 all-reduce.9
  592.2 120.2 all-reduce.11
Sparse Core Ops, SparseCore 1:
  90.4 25.2 all-gather.9
  118.0 23.8 all-gather.11
  379.6 32.5 reduce-scatter.23
  416.1 42.2 reduce-scatter.17
  462.2 42.2 reduce-scatter.15
  566.2 33.9 reduce-scatter.21
  603.5 40.0 reduce-scatter.19
  719.0 32.9 reduce-scatter.25
where the time goes:
time: 772 us; the launch traced here: 761 us
  waiting for transfers between devices  423 us (55%)
  matrix products  94.3 us (12%)
  local copies, waits for them, and re-layouts  90.2 us (12%)
  blocking collectives  71.4 us (9%)
  other arithmetic  63 us (8%)
  between operations  17.6 us (2%)
    psum x1, waiting for transfers between devices, body(): ffn = lax.psum(ffn_part.astype(jnp.bfloat16), 'tensor').astype(jnp.float32)  120 us
    psum x1, waiting for transfers between devices, body(): lax.psum(feed_part.astype(jnp.bfloat16), 'tensor').astype(jnp.float32)  103 us
    psum x1, waiting for transfers between devices, body(): lax.psum(attn_part.astype(jnp.bfloat16), 'tensor').astype(jnp.float32)  81.6 us
    psum x1, waiting for transfers between devices, body(): lax.psum(input_part.astype(jnp.bfloat16), 'tensor').astype(jnp.float32)  67.8 us
    unnamed x16, waiting for transfers between devices  50.9 us
    unnamed x98, local copies, waits for them, and re-layouts  29.5 us
    reduce_sum x4, other arithmetic, layer_norm(): center = value - jnp.mean(value, axis=-1, keepdims=True)  18.3 us
    dot_general x2, matrix products, contract_rows(): lax.dot_general(left, right, (((0,), (0,)), ((), ())), preferred_element_...  16 us
  transfers between devices with their start and end apart: 12, of which 6 were waited for; matrix products, arithmetic and copies ran while one was open for 21% of the time, Pallas kernels for 0%

commit v1 on v0

--- a/solution.py
+++ b/solution.py
@@ -10,6 +10,27 @@
 beta_second = 0.999
 warm_steps = 10000.0
 total_steps = 200000.0
+
+
+def joined_along(blocks, dim):
+    blocks = jnp.moveaxis(blocks, 0, dim)
+    shape = blocks.shape
+    return blocks.reshape(*shape[:dim], shape[dim] * shape[dim + 1], *shape[dim + 2 :])
+
+
+def grow_blocks(shard, axis):
+    size, here = (lax.axis_size(axis), lax.axis_index(axis))
+    blocks, bit = (shard[None], 1)
+    while bit < size:
+        other = lax.ppermute(blocks, axis, [(i, i ^ bit) for i in range(size)])
+        low = here & bit == 0
+        blocks = jnp.concatenate([jnp.where(low, blocks, other), jnp.where(low, other, blocks)])
+        bit *= 2
+    return blocks
+
+
+def collect(x, axis, dim):
+    return joined_along(grow_blocks(x, axis), dim)
 
 
 def layer_norm(value, gain, shift):
@@ -64,7 +85,7 @@
     bf = jnp.bfloat16
     fl = jnp.float32
     w_qkv, b_qv, w_out, w_up, b_up, w_down, vectors = (
-        lax.all_gather(qkv_state[0].astype(bf), "dp", axis=0, tiled=True),
+        collect(qkv_state[0].astype(bf), "dp", 0),
         lax.all_gather(qv_bias_state[0].astype(bf), "dp", axis=2, tiled=True),
         lax.all_gather(out_state[0].astype(bf), "dp", axis=1, tiled=True),
         lax.all_gather(up_state[0].astype(bf), "dp", axis=0, tiled=True),

time: 772 us -> 776 us (level)
  blocking collectives: 71.4 us -> 55.7 us
  waiting for transfers between devices: 423 us -> 438 us
    all_gather x1 -> x0, blocking collectives: 15.8 us -> none  [body(): lax.all_gather(qkv_state[0].astype(bf), 'dp', axis=0, tiled=True)]
    ppermute x0 -> x3, waiting for transfers between devices: none -> 13.5 us  [grow_blocks(): other = lax.ppermute(blocks, axis, [(i, i ^ bit) for i in range(size)])]
    unnamed x98 -> x104, local copies, waits for them, and re-layouts: 29.5 us -> 30.1 us
  transfers between devices with their start and end apart: 12 -> 15, of which waited for: 6 -> 7; matrix products, arithmetic and copies ran while one was open for 21% -> 22% of each run, Pallas kernels for 0% -> 0%
where the time goes in v1:
time: 776 us; the launch traced here: 766 us
  waiting for transfers between devices  438 us (56%)
  matrix products  96.2 us (12%)
  local copies, waits for them, and re-layouts  90.2 us (12%)
  other arithmetic  65.3 us (8%)
  blocking collectives  55.7 us (7%)
  between operations  17.6 us (2%)
    psum x1, waiting for transfers between devices, body(): ffn = lax.psum(ffn_part.astype(jnp.bfloat16), 'tensor').astype(jnp.float32)  120 us
    psum x1, waiting for transfers between devices, body(): lax.psum(feed_part.astype(jnp.bfloat16), 'tensor').astype(jnp.float32)  103 us
    psum x1, waiting for transfers between devices, body(): lax.psum(attn_part.astype(jnp.bfloat16), 'tensor').astype(jnp.float32)  82.3 us
    psum x1, waiting for transfers between devices, body(): lax.psum(input_part.astype(jnp.bfloat16), 'tensor').astype(jnp.float32)  67.7 us
    unnamed x16, waiting for transfers between devices  50.9 us
    unnamed x104, local copies, waits for them, and re-layouts  30.1 us
    reduce_sum x4, other arithmetic, layer_norm(): center = value - jnp.mean(value, axis=-1, keepdims=True)  18.4 us
    dot_general x2, matrix products, contract_rows(): lax.dot_general(left, right, (((0,), (0,)), ((), ())), preferred_element_...  16 us
  transfers between devices with their start and end apart: 15, of which 7 were waited for; matrix products, arithmetic and copies ran while one was open for 22% of the time, Pallas kernels for 0%

profile of v1, /device:TPU:0, one launch (start us, length us, event | category | flops | bytes accessed | tf_op | source)
XLA Modules:
  0.0 766.1 jit_solution(15131227517994452526)
XLA Ops:
  10.4 10.1 %all-gather = bf16[1,2,3,64]{2,1,0,3:T(2,128)(2,1)S(1)} all-gather(bf16[1,2,3,8]{2,1,0,3:T(2,128)(2,1)S(1)} %copy.178), channel_id=2, replica_groups=mesh['dp'=8,'tensor'=4] {'dp'}, dimensions={3}, use_global_device_ids=true | all-gather | bytes 864 | tf_op jit(solution)/shard_map/all_gather | solution.py:89
  23.0 1.5 collective-permute-start.1
  25.9 12.6 %all-gather.1 = bf16[1,192,768]{1,0,2:T(2,128)(2,1)S(1)} all-gather(bf16[1,192,96]{1,0,2:T(2,128)(2,1)S(1)} %copy.139), channel_id=3, replica_groups=mesh['dp'=8,'tensor'=4] {'dp'}, dimensions={2}, use_global_device_ids=true | all-gather | bytes 331776 | tf_op jit(solution)/shard_map/all_gather | solution.py:90
  39.0 1.3 broadcast_select_fusion.3
  41.1 1.5 broadcast_compare_fusion
  42.6 13.4 %collective-permute-done.2 = bf16[4,96,3,192]{3,1,2,0:T(8,128)(2,1)S(1)} collective-permute-done((bf16[4,96,3,192]{3,1,2,0:T(8,128)(2,1)S(1)}, bf16[4,96,3,192]{3,1,2,0:T(8,128)(2,1)S(1)}, u32[]{:S(2)}, u32[]{:S(2)}) %collective-permute-start.2) | collective-permute-done | bytes 442400 | tf_op jit(solution)/shard_map/ppermute | solution.py:25
  57.4 2.6 copy.130
  60.0 2.9 reshape.217
  62.9 4.6 fusion.13
  67.5 6.2 reshape.218
  73.6 2.4 fusion.69
  76.1 4.4 fusion.73
  80.5 1.8 fusion
  82.4 2.8 copy-done
  85.3 2.8 fusion.23
  89.8 2.7 convolution_convert_fusion.2
  92.6 1.6 slice.205
  94.3 1.6 slice.204
  98.2 8.4 %all-gather.4 = bf16[1,6,128]{1,0,2:T(2,128)(2,1)S(1)} all-gather(bf16[1,6,16]{1,0,2:T(2,128)(2,1)} %copy.142), channel_id=6, replica_groups=mesh['dp'=8,'tensor'=4] {'dp'}, dimensions={2}, use_global_device_ids=true | all-gather | bytes 1728 | tf_op jit(solution)/shard_map/all_gather | solution.py:92
  108.0 10.3 %all-gather.2 = bf16[1,6,768]{1,0,2:T(2,128)(2,1)S(1)} all-gather(bf16[1,6,96]{1,0,2:T(2,128)(2,1)S(1)} %copy.182), channel_id=4, replica_groups=mesh['dp'=8,'tensor'=4] {'dp'}, dimensions={2}, use_global_device_ids=true | all-gather | bytes 10368 | tf_op jit(solution)/shard_map/all_gather | solution.py:94
  118.7 13.0 %slice_reduce_fusion.1 = (f32[768]{0:T(1024)S(1)}, f32[768]{0:T(1024)S(1)}, f32[768]{0:T(1024)S(1)}, f32[768]{0:T(1024)S(1)}, f32[768]{0:T(1024)S(1)}, /*index=5*/f32[768]{0:T(1024)S(1)}) fusion(f32[1,6,768]{1,0,2:T(1,128)S(1)} %convert_element_type.170), kind=kLoop, calls=%fused_computation.82 | loop fusion | bytes 36864 | tf_op jit(solution)/shard_map/slice | solution.py:133
  131.7 82.3 %all-reduce.6.cloned.1.call-done = bf16[2048,768]{1,0:T(8,128)(2,1)} async-done(((bf16[2048,768]{1,0:T(8,128)(2,1)}), bf16[2048,768]{1,0:T(8,128)(2,1)}) %all-reduce.6.cloned.1.call-update) | async-done | bytes 3145744 | tf_op jit(solution)/shard_map/psum | solution.py:125
  214.0 3.1 fusion.11
  217.1 3.6 multiply_reduce_fusion.4
  220.8 7.4 multiply_convert_fusion.1
  228.3 6.2 convolution_convert_fusion.1
  234.5 120.2 %all-reduce.8.cloned.1.call-done = bf16[2048,768]{1,0:T(8,128)(2,1)} async-done(((bf16[2048,768]{1,0:T(8,128)(2,1)}), bf16[2048,768]{1,0:T(8,128)(2,1)}) %all-reduce.8.cloned.1.call-update) | async-done | bytes 3145744 | tf_op jit(solution)/shard_map/psum | solution.py:132
  354.7 4.9 fusion.67
  361.5 3.0 fusion.7
  364.6 4.3 fusion.66
  369.0 5.9 convert_reduce_fusion.1
  374.9 1.7 copy-done.38
  376.7 4.0 convolution_convert_fusion
  381.6 8.0 %fusion.60 = f32[768,768]{0,1:T(8,128)} fusion(bf16[2048,768]{1,0:T(8,128)(2,1)} %copy-done.39, f32[2048,768]{1,0:T(8,128)} %copy-done.2, f32[2048]{0:T(1024)S(1)} %negate_multiply_fusion.1), kind=kOutput, calls=%fused_computation.156 | convolution fusion | flops 2419064832 | bytes 11804672 | tf_op jit(solution)/shard_map/dot_general | solution.py:55
  389.7 8.0 %fusion.61 = f32[768,768]{1,0:T(8,128)} fusion(bf16[2048,768]{1,0:T(8,128)(2,1)} %copy-done.38, f32[2048,768]{1,0:T(8,128)} %get-tuple-element.123, f32[768]{0:T(1024)} %copy-done.27, f32[768]{0:T(1024)} %copy-done.24, f32[2048]{0:T(1024)S(1)} %fusion.49), kind=kOutput, calls=%fused_computation.157 | convolution fusion | flops 2422210560 | bytes 11810816 | tf_op jit(solution)/shard_map/dot_general | solution.py:55
  397.8 103.1 %all-reduce.10.cloned.1.call-done = bf16[2048,768]{1,0:T(8,128)(2,1)} async-done(((bf16[2048,768]{1,0:T(8,128)(2,1)}), bf16[2048,768]{1,0:T(8,128)(2,1)}) %all-reduce.10.cloned.1.call-update) | async-done | bytes 3145744 | tf_op jit(solution)/shard_map/psum | solution.py:142
  500.9 8.2 %multiply_reduce_fusion.1 = (f32[768]{0:T(1024)}, f32[2048]{0:T(1024)S(1)}, f32[768]{0:T(1024)}, f32[768]{0:T(1024)}) fusion(f32[2048,768]{1,0:T(8,128)} %get-tuple-element.123, f32[2048]{0:T(1024)S(1)} %fusion.49, bf16[2048,768]{1,0:T(8,128)(2,1)} %all-reduce.10.cloned.1.call-done, f32[2048,768]{1,0:T(8,128)} %copy-done.2, ...), kind=kLoop, calls=%fused_computation.19 | loop fusion | flops 17297152 | bytes 15765504 | tf_op jit(solution)/shard_map/transpose(jvp())/reduce_sum | solution.py:39
  509.1 6.1 fusion.65
  515.2 2.6 copy-done.3
  517.8 2.2 convolution_convert_fusion.3
  520.0 3.0 reshape.221
  523.0 8.3 %multiply_reduce_fusion = (f32[4,3,512]{2,1,0:T(4,128)S(1)}, f32[4,3,512,512]{2,3,1,0:T(8,128)S(1)}) fusion(f32[4,3,512,512]{2,3,1,0:T(8,128)} %copy-done, f32[4,3,512]{2,1,0:T(4,128)S(1)} %log_add_fusion, bf16[4,512,1,3,64]{1,0,4,3,2:T(4,128)(2,1)} %copy-done.11, bf16[4,512,3,64]{1,0,3,2:T(4,128)(2,1)} %reshape.221), kind=kOutput, calls=%fused_computation.1 | convolution fusion | flops 412084224 | bytes 26787840 | tf_op jit(solution)/shard_map/bqhd,bkhd->bhqk/dot_general | solution.py:153
  531.3 6.9 multiply_convert_fusion
  538.2 2.6 copy-done.1
  541.9 1.5 copy.146
  543.4 3.2 stack.101
  546.6 5.1 fusion.22
  551.7 1.5 copy.148
  553.2 2.8 stack.102
  556.0 2.1 constant_dynamic-update-slice_fusion.2
  558.1 5.6 convolution_bitcast_fusion
  563.7 7.8 %fusion.18 = bf16[4,512,3,64]{1,3,2,0:T(8,128)(2,1)} fusion(f32[4,3,512,512]{2,3,1,0:T(8,128)} %copy-done, f32[4,3,512]{2,1,0:T(4,128)S(1)} %log_add_fusion, bf16[4,512,3,64]{1,0,3,2:T(4,128)(2,1)} %reshape.221), kind=kOutput, calls=%fused_computation.54 | convolution fusion | flops 409337856 | bytes 14180352 | tf_op jit(solution)/shard_map/bhqk,bqhd->bkhd/dot_general | solution.py:154
  571.6 2.1 constant_dynamic-update-slice_fusion.1
  573.6 2.6 copy.151
  576.3 2.8 stack.103
  579.1 2.1 constant_dynamic-update-slice_fusion
  581.2 5.8 fusion.74
  587.0 2.8 copy.176
  591.2 6.2 bitcast_convert_fusion
  606.9 14.3 %all-reduce = f32[2,3,64]{2,1,0:T(4,128)S(1)} all-reduce(f32[2,3,64]{2,1,0:T(4,128)S(1)} %reshape.223), channel_id=9, replica_groups=mesh['dp'=8,'tensor'=4] {'dp'}, use_global_device_ids=true, to_apply=%region_17.18.clone | all-reduce | flops 384 | bytes 3072
  629.2 19.7 %reduce-scatter.20.cloned.1.call-done = f32[96,576]{1,0:T(8,128)} async-done(((f32[768,576]{1,0:T(8,128)}), f32[96,576]{1,0:T(8,128)}) %reduce-scatter.20.cloned.1.call-update) | async-done | bytes 221200
  650.1 67.7 %all-reduce.12.cloned.1.call-done = bf16[2048,768]{1,0:T(8,128)(2,1)} async-done(((bf16[2048,768]{1,0:T(8,128)(2,1)}), bf16[2048,768]{1,0:T(8,128)(2,1)}) %all-reduce.12.cloned.1.call-update) | async-done | bytes 3145744 | tf_op jit(solution)/shard_map/psum | solution.py:173
  717.9 5.4 add_reduce_fusion
  726.3 31.0 %reduce-scatter.26.cloned.1.call-done = f32[96,6]{1,0:T(8,128)} async-done(((f32[768,6]{1,0:T(8,128)}), f32[96,6]{1,0:T(8,128)}) %reduce-scatter.26.cloned.1.call-update) | async-done | bytes 2320
  (196 shorter events, 42.0 us)
Async XLA Ops:
  8.0 33.1 %copy-start.26 = (s32[4,512]{1,0:T(4,128)S(1)}, s32[4,512]{1,0:T(4,128)}, u32[]{:S(2)}) copy-start(s32[4,512]{1,0:T(4,128)} %param.13) | copy-start | bytes 24580
  8.0 205.9 %all-reduce.6.cloned.1.call-start = ((), (), s32[]{:S(2)}) async-start(), calls=%async_computation.6 | async-start | bytes 6291456 | tf_op jit(solution)/shard_map/psum | solution.py:125
  9.1 11.5 %collective-permute-start = (bf16[1,96,3,192]{3,1,2,0:T(8,128)(2,1)S(1)}, bf16[1,96,3,192]{3,1,2,0:T(8,128)(2,1)S(1)}, u32[]{:S(2)}, u32[]{:S(2)}) collective-permute-start(bf16[1,96,3,192]{3,1,2,0:T(8,128)(2,1)S(1)} %slice.206), channel_id=1, source_target_pairs={{0,4},{4,0},{8,12},{12,8},{16,20},{20,16},{24,28},{28,24},{1,5},{5... | collective-permute-start | bytes 331784 | tf_op jit(solution)/shard_map/ppermute | solution.py:25
  21.5 0.7 copy-start.14
  21.5 1.4 copy-start.15
  23.0 16.0 %collective-permute-start.1 = (bf16[2,96,3,192]{3,1,2,0:T(8,128)(2,1)}, bf16[2,96,3,192]{3,1,2,0:T(8,128)(2,1)}, u32[]{:S(2)}, u32[]{:S(2)}) collective-permute-start(bf16[2,96,3,192]{3,1,2,0:T(8,128)(2,1)} %pad_maximum_fusion.5), channel_id=1, source_target_pairs={{0,8},{4,12},{8,0},{12,4},{16,24},{20,28},{24,16},{28,20},{1,9},{5... | collective-permute-start | bytes 663560 | tf_op jit(solution)/shard_map/ppermute | solution.py:25
  39.0 23.9 %copy-start.6 = (bf16[4,512,768]{2,1,0:T(8,128)(2,1)S(1)}, bf16[4,512,768]{2,1,0:T(8,128)(2,1)}, u32[]{:S(2)}) copy-start(bf16[4,512,768]{2,1,0:T(8,128)(2,1)} %param.11) | copy-start | bytes 9437188
  40.4 15.7 %collective-permute-start.2 = (bf16[4,96,3,192]{3,1,2,0:T(8,128)(2,1)S(1)}, bf16[4,96,3,192]{3,1,2,0:T(8,128)(2,1)S(1)}, u32[]{:S(2)}, u32[]{:S(2)}) collective-permute-start(bf16[4,96,3,192]{3,1,2,0:T(8,128)(2,1)S(1)} %pad_maximum_fusion.1), channel_id=1, source_target_pairs={{0,16},{4,20},{8,24},{12,28},{16,0},{20,4},{24,8},{28,12},{1,17},{... | collective-permute-start | bytes 1327112 | tf_op jit(solution)/shard_map/ppermute | solution.py:25
  76.1 4.4 copy-start.9
  76.1 4.4 copy-start.12
  76.1 6.3 copy-start.11
  80.5 4.7 copy-start
  80.5 4.7 copy-start.18
  82.3 5.8 copy-start.20
  88.9 0.9 copy-start.8
  92.5 128.3 %all-gather.9.cloned.1.call-start = ((), (), s32[]{:S(2)}) async-start(), calls=%async_computation.12 | async-start | bytes 1327104 | tf_op jit(solution)/shard_map/all_gather | solution.py:91
  94.2 134.1 %all-gather.11.cloned.1.call-start = ((), (), s32[]{:S(2)}) async-start(), calls=%async_computation.13 | async-start | bytes 1327104 | tf_op jit(solution)/shard_map/all_gather | solution.py:93
  95.9 258.8 %all-reduce.8.cloned.1.call-start = ((), (), s32[]{:S(2)}) async-start(), calls=%async_computation.7 | async-start | bytes 6291456 | tf_op jit(solution)/shard_map/psum | solution.py:132
  131.7 223.0 %copy-start.24 = (f32[768]{0:T(1024)}, f32[768]{0:T(1024)S(1)}, u32[]{:S(2)}) copy-start(f32[768]{0:T(1024)S(1)} %get-tuple-element.111) | copy-start | bytes 9220
  131.7 223.0 %copy-start.27 = (f32[768]{0:T(1024)}, f32[768]{0:T(1024)S(1)}, u32[]{:S(2)}) copy-start(f32[768]{0:T(1024)S(1)} %get-tuple-element.110) | copy-start | bytes 9220
  214.0 3.2 copy-start.7
  220.8 7.5 copy-start.22
  228.3 6.2 copy-start.39
  234.5 266.4 %all-reduce.10.cloned.1.call-start = ((), (), s32[]{:S(2)}) async-start(), calls=%async_computation.8 | async-start | bytes 6291456 | tf_op jit(solution)/shard_map/psum | solution.py:142
  359.6 1.9 copy-start.4
  361.5 7.4 slice-start
  364.6 4.3 copy-start.37
  364.6 4.3 slice-start.1
  368.9 6.0 copy-start.2
  369.0 7.7 %copy-start.36 = (bf16[1,768,768]{2,1,0:T(8,128)(2,1)S(1)}, bf16[1,768,768]{2,1,0:T(8,128)(2,1)}, u32[]{:S(2)}) copy-start(bf16[1,768,768]{2,1,0:T(8,128)(2,1)} %all-gather.9.cloned.1.call-done) | copy-start | bytes 3538948
  374.9 1.8 copy-start.38
  380.7 222.2 %reduce-scatter.24.cloned.1.call-start = ((), (), s32[]{:S(2)}) async-start(), calls=%async_computation.16 | async-start | bytes 73728
  381.5 8.1 %copy-start.19 = (f32[4,3,512]{2,1,0:T(4,128)S(1)}, f32[4,3,512]{2,1,0:T(4,128)}, u32[]{:S(2)}) copy-start(f32[4,3,512]{2,1,0:T(4,128)} %copy-done.18) | copy-start | bytes 73732
  381.5 8.1 %copy-start.21 = (f32[4,3,512]{2,1,0:T(4,128)S(1)}, f32[4,3,512]{2,1,0:T(4,128)}, u32[]{:S(2)}) copy-start(f32[4,3,512]{2,1,0:T(4,128)} %copy-done.20) | copy-start | bytes 73732
  381.5 241.7 %reduce-scatter.18.cloned.1.call-start = ((), (), s32[]{:S(2)}) async-start(), calls=%async_computation.11 | async-start | bytes 2654208 | tf_op jit(solution)/shard_map/reduce_scatter | solution.py:182
  389.6 235.8 %reduce-scatter.16.cloned.1.call-start = ((), (), s32[]{:S(2)}) async-start(), calls=%async_computation.10 | async-start | bytes 2654208 | tf_op jit(solution)/shard_map/reduce_scatter | solution.py:180
  389.7 111.2 %copy-start.25 = (f32[768]{0:T(1024)S(1)}, f32[768]{0:T(1024)}, u32[]{:S(2)}) copy-start(f32[768]{0:T(1024)} %copy-done.24) | copy-start | bytes 9220
  397.7 111.4 %copy-start.23 = (f32[2048]{0:T(1024)S(1)}, f32[2048]{0:T(1024)}, u32[]{:S(2)}) copy-start(f32[2048]{0:T(1024)} %copy-done.22) | copy-start | bytes 24580
  397.7 229.7 %reduce-scatter.22.cloned.1.call-start = ((), (), s32[]{:S(2)}) async-start(), calls=%async_computation.15 | async-start | bytes 884736
  500.9 8.2 %copy-start.5 = (bf16[2048,768]{1,0:T(8,128)(2,1)S(1)}, bf16[2048,768]{1,0:T(8,128)(2,1)}, u32[]{:S(2)}) copy-start(bf16[2048,768]{1,0:T(8,128)(2,1)} %all-reduce.10.cloned.1.call-done) | copy-start | bytes 9437188
  515.2 2.6 copy-start.3
  531.3 9.5 %copy-start.13 = (bf16[4,512,1,3,64]{1,0,4,3,2:T(4,128)(2,1)S(1)}, bf16[4,512,1,3,64]{1,0,4,3,2:T(4,128)(2,1)}, u32[]{:S(2)}) copy-start(bf16[4,512,1,3,64]{1,0,4,3,2:T(4,128)(2,1)} %copy-done.12) | copy-start | bytes 2359300
  538.2 2.6 copy-start.1
  571.5 77.4 %reduce-scatter.20.cloned.1.call-start = ((), (), s32[]{:S(2)}) async-start(), calls=%async_computation.14 | async-start | bytes 2211840
  589.9 128.0 %all-reduce.12.cloned.1.call-start = ((), (), s32[]{:S(2)}) async-start(), calls=%async_computation.9 | async-start | bytes 6291456 | tf_op jit(solution)/shard_map/psum | solution.py:173
  591.2 8.3 %copy-start.30 = (f32[768]{0:T(1024)S(1)}, f32[768]{0:T(1024)}, u32[]{:S(2)}) copy-start(f32[768]{0:T(1024)} %convert_reduce_fusion) | copy-start | bytes 9220
  591.2 11.7 %copy-start.28 = (f32[768]{0:T(1024)S(1)}, f32[768]{0:T(1024)}, u32[]{:S(2)}) copy-start(f32[768]{0:T(1024)} %get-tuple-element.104) | copy-start | bytes 9220
  591.2 15.2 %copy-start.29 = (f32[768]{0:T(1024)S(1)}, f32[768]{0:T(1024)}, u32[]{:S(2)}) copy-start(f32[768]{0:T(1024)} %get-tuple-element.107) | copy-start | bytes 9220
  597.4 9.0 %copy-start.10 = (bf16[2048,3,192]{0,2,1:T(8,128)(2,1)S(1)}, bf16[2048,3,192]{0,2,1:T(8,128)(2,1)}, u32[]{:S(2)}) copy-start(bf16[2048,3,192]{0,2,1:T(8,128)(2,1)} %constant_dynamic-update-slice_fusion) | copy-start | bytes 7077892
  597.5 31.0 %copy-start.17 = (f32[3,192,96]{2,1,0:T(8,128)S(1)}, f32[3,192,96]{2,1,0:T(8,128)}, u32[]{:S(2)}) copy-start(f32[3,192,96]{2,1,0:T(8,128)} %param.17) | copy-start | bytes 663556
  597.5 159.8 %reduce-scatter.26.cloned.1.call-start = ((), (), s32[]{:S(2)}) async-start(), calls=%async_computation.17 | async-start | bytes 442368
  603.7 119.5 %copy-start.31 = (f32[6,16]{1,0:T(8,128)}, f32[6,16]{1,0:T(8,128)S(1)}, u32[]{:S(2)}) copy-start(f32[6,16]{1,0:T(8,128)S(1)} %copy.173) | copy-start | bytes 1156
  622.0 101.3 %copy-start.33 = (f32[2,3,8]{2,0,1:T(2,128)}, f32[2,3,8]{2,0,1:T(2,128)S(1)}, u32[]{:S(2)}) copy-start(f32[2,3,8]{2,0,1:T(2,128)S(1)} %get-tuple-element.115) | copy-start | bytes 580
  628.5 94.8 %copy-start.16 = (f32[192,96]{1,0:T(8,128)}, f32[192,96]{1,0:T(8,128)S(1)}, u32[]{:S(2)}) copy-start(f32[192,96]{1,0:T(8,128)S(1)} %copy.171) | copy-start | bytes 221188
  650.1 73.2 %copy-start.34 = (f32[1,768]{1,0:T(1,128)S(1)}, f32[1,768]{1,0:T(1,128)}, u32[]{:S(2)}) copy-start(f32[1,768]{1,0:T(1,128)} %reshape.228) | copy-start | bytes 9220
  650.1 108.0 %copy-start.35 = (f32[3,6,96]{2,1,0:T(8,128)S(1)}, f32[3,6,96]{2,1,0:T(8,128)}, u32[]{:S(2)}) copy-start(f32[3,6,96]{2,1,0:T(8,128)} %param.21) | copy-start | bytes 20740
  758.2 0.6 copy-start.32
Sparse Core Ops, SparseCore 0:
  92.6 121.2 all-reduce.5
  234.6 120.0 all-reduce.7
  380.8 120.0 all-reduce.9
  597.6 120.2 all-reduce.11
Sparse Core Ops, SparseCore 1:
  95.5 25.1 all-gather.8
  122.9 23.8 all-gather.10
  384.8 32.5 reduce-scatter.23
  421.2 42.2 reduce-scatter.17
  467.4 42.2 reduce-scatter.15
  571.6 33.9 reduce-scatter.21
  608.8 40.0 reduce-scatter.19
  724.4 32.9 reduce-scatter.25
